TPU v7x, 256 devices: a whole 4x4x8 slice. The times are simulated.
256 devices in a mesh: seq: 64 (over x, z_hi, y), heads: 4 (over z_lo, core).
Axes of the slice: x: 4, y: 4, z: 8 (z_hi: 4, z_lo: 2; z = z_hi * 2 + z_lo), core: 2. Of those that a mesh axis runs over, the one named last changes fastest.
Arguments:
- queries: bfloat16 [131072, 2048], P('seq', 'heads'), may hold values from -120 to 120
- keys: bfloat16 [512, 2048], P(None, 'heads'), may hold values from -4.2 to 4.2
- values: bfloat16 [512, 2048], P(None, 'heads'), may hold values from -6 to 6
- out_grad: bfloat16 [131072, 2048], P('seq', 'heads'), may hold values from -6 to 6
- key_proj: bfloat16 [2048, 2048], P(None, 'heads'), may hold values from -0.125 to 0.125
- value_proj: bfloat16 [2048, 2048], P(None, 'heads'), may hold values from -0.125 to 0.125
- global_in: bfloat16 [512, 2048], P('seq', 'heads'), may hold values from -6 to 6
- up_proj: bfloat16 [2048, 8192], P('heads', 'seq'), may hold values from -0.125 to 0.125
- down_proj: bfloat16 [8192, 2048], P('seq', 'heads'), may hold values from -0.0625 to 0.0625
Outputs:
- query_grad: bfloat16 [131072, 2048], P('seq', 'heads')
- global_grad: float32 [512, 2048], P('seq', 'heads')
All inputs are finite; a program needn't handle non-finite values.
Results may differ from a plain program's by a relative error of at most 0.014.
Values may be sent and summed in bfloat16 or wider, within the bound.
A program may use at most 128 MiB of HBM per device.

v0:
```python
import jax
import jax.numpy as jnp
from jax import lax
from jax.sharding import PartitionSpec as P

HD = 128


def slope_of(pre):
    return (
        0.5 * (1.0 + lax.erf(pre * 0.7071067811865476))
        + pre * jnp.exp(-0.5 * pre * pre) * 0.3989422804014327
    )


def project(key_sum, value_sum, key_proj, value_proj):
    first = jnp.einsum(
        "gc,dc->gd", key_sum.astype(jnp.bfloat16), key_proj, preferred_element_type=jnp.float32
    )
    second = jnp.einsum(
        "gc,dc->gd", value_sum.astype(jnp.bfloat16), value_proj, preferred_element_type=jnp.float32
    )
    return first + second


def local(queries, keys, values, out_grad, key_proj, value_proj, global_in, up_proj, down_proj):
    tok_rows, width = queries.shape
    glob_rows = keys.shape[0]
    local_heads = width // HD
    scale = HD ** (-0.5)
    block = min(512, tok_rows)
    blocks = tok_rows // block
    pre_part = jnp.dot(
        lax.all_gather(global_in, "seq", axis=0, tiled=True),
        up_proj,
        preferred_element_type=jnp.float32,
    )
    key_heads = keys.reshape(glob_rows, local_heads, HD)
    value_heads = values.reshape(glob_rows, local_heads, HD)
    query_blocks = queries.reshape(blocks, block, local_heads, HD)
    grad_blocks = out_grad.reshape(blocks, block, local_heads, HD)

    def attend(carry, pair):
        key_total, value_total = carry
        query_block, grad_block = pair
        scores = scale * jnp.einsum(
            "rhd,ghd->hrg", query_block, key_heads, preferred_element_type=jnp.float32
        )
        weights = jax.nn.softmax(scores, axis=-1)
        weight_grad = jnp.einsum(
            "rhd,ghd->hrg", grad_block, value_heads, preferred_element_type=jnp.float32
        )
        centre = jnp.sum(weights * weight_grad, axis=-1, keepdims=True)
        score_grad = (weights * (weight_grad - centre)).astype(jnp.bfloat16)
        weights_low = weights.astype(jnp.bfloat16)
        block_grad = (
            scale
            * jnp.einsum("hrg,ghd->rhd", score_grad, key_heads, preferred_element_type=jnp.float32)
        ).astype(jnp.bfloat16)
        key_total = key_total + jnp.einsum(
            "hrg,rhd->ghd", score_grad, query_block, preferred_element_type=jnp.float32
        )
        value_total = value_total + jnp.einsum(
            "hrg,rhd->ghd", weights_low, grad_block, preferred_element_type=jnp.float32
        )
        return ((key_total, value_total), block_grad)

    empty = jnp.zeros((glob_rows, local_heads, HD), jnp.float32)
    (key_total, value_total), block_grads = lax.scan(
        attend, (empty, empty), (query_blocks, grad_blocks)
    )
    query_grad = block_grads.reshape(tok_rows, width)
    key_total = scale * key_total.reshape(glob_rows, width)
    value_total = value_total.reshape(glob_rows, width)
    key_sum, value_sum = lax.psum((key_total, value_total), "seq")
    state_share = lax.psum_scatter(
        project(key_sum, value_sum, key_proj, value_proj).astype(jnp.bfloat16),
        "heads",
        scatter_dimension=1,
        tiled=True,
    ).astype(jnp.float32)
    state_low = state_share.astype(jnp.bfloat16)
    share_rows = glob_rows // lax.axis_size("seq")
    own_state = lax.dynamic_slice_in_dim(
        state_share, lax.axis_index("seq") * share_rows, share_rows, 0
    )
    back_part = jnp.einsum("gc,fc->gf", state_low, down_proj, preferred_element_type=jnp.float32)
    pre_total, back_total = (
        lax.psum(pre_part.astype(jnp.bfloat16), "heads").astype(jnp.float32),
        lax.psum(back_part.astype(jnp.bfloat16), "heads").astype(jnp.float32),
    )
    gated = (slope_of(pre_total) * back_total).astype(jnp.bfloat16)
    input_part = jnp.einsum("gf,cf->gc", gated, up_proj, preferred_element_type=jnp.float32)
    global_grad = own_state + lax.psum_scatter(input_part, "seq", scatter_dimension=0, tiled=True)
    return (query_grad, global_grad)


def solution(mesh):
    placed = (
        P("seq", "heads"),
        P(None, "heads"),
        P(None, "heads"),
        P("seq", "heads"),
        P(None, "heads"),
        P(None, "heads"),
        P("seq", "heads"),
        P("heads", "seq"),
        P("seq", "heads"),
    )
    return jax.shard_map(
        local,
        mesh=mesh,
        in_specs=placed,
        out_specs=(P("seq", "heads"), P("seq", "heads")),
        check_vma=False,
    )
```

profile of v0, /device:TPU:0, one launch (start us, length us, event | category | flops | bytes accessed | tf_op | source)
XLA Modules:
  0.0 1139.3 jit_solution(193295031529866412)
XLA Ops:
  7.2 0.0 reduce-scatter.3.cloned.1.call-start
  7.3 1.4 copy.22
  8.6 0.3 copy.25
  8.9 1.3 copy.23
  10.2 1.0 copy.27
  11.2 4.0 reshape.28
  15.2 4.0 reshape.30
  19.2 83.3 %while.15 = (s32[]{:T(128)}, f32[512,4,128]{0,2,1:T(8,128)}, f32[512,4,128]{0,2,1:T(8,128)}, bf16[4,512,4,128]{3,2,1,0:T(4,128)(2,1)}, bf16[4,512,4,128]{3,2,1,0...) while((s32[]{:T(128)}, f32[512,4,128]{0,2,1:T(8,128)}, ...), condition=%wide.region_4.5_spmd.clone, body=%wide.region_0.4_spmd.clone.sunk | while | flops 1360528384 | bytes 93372648 | solution.py:69
  19.2 2.4 constant_dynamic-slice_fusion.3
  21.5 0.7 fusion.81
  22.3 3.2 fusion.82
  25.5 6.4 fusion.84
  31.8 3.4 multiply_reduce_fusion.3
  35.2 0.4 copy-done.1
  35.6 1.2 multiply_convert_fusion.2
  36.8 0.0 copy-done.3
  36.8 0.9 fusion.83
  37.7 0.9 fusion.85
  38.6 1.2 copy_dynamic-update-slice_fusion.2
  39.9 2.4 constant_dynamic-slice_fusion.3
  42.2 0.7 fusion.81
  43.0 3.2 fusion.82
  46.1 6.6 fusion.84
  52.7 3.4 multiply_reduce_fusion.3
  56.1 0.4 copy-done.1
  56.5 1.2 multiply_convert_fusion.2
  57.7 0.9 fusion.83
  58.6 0.9 fusion.85
  59.5 1.2 copy_dynamic-update-slice_fusion.2
  60.7 2.4 constant_dynamic-slice_fusion.3
  63.1 0.7 fusion.81
  63.8 3.2 fusion.82
  67.0 6.6 fusion.84
  73.6 3.4 multiply_reduce_fusion.3
  77.0 0.4 copy-done.1
  77.3 1.2 multiply_convert_fusion.2
  78.6 0.9 fusion.83
  79.5 0.9 fusion.85
  80.4 1.2 copy_dynamic-update-slice_fusion.2
  81.6 2.4 constant_dynamic-slice_fusion.3
  84.0 0.7 fusion.81
  84.7 3.2 fusion.82
  87.9 6.6 fusion.84
  94.4 3.4 multiply_reduce_fusion.3
  97.8 0.4 copy-done.1
  98.2 1.2 multiply_convert_fusion.2
  99.4 0.9 fusion.83
  100.3 0.9 fusion.85
  101.3 1.2 copy_dynamic-update-slice_fusion.2
  102.5 2.3 broadcast_multiply_fusion
  104.8 403.6 %all-reduce.6 = (bf16[512,512]{0,1:T(8,128)(2,1)S(1)}, bf16[512,512]{0,1:T(8,128)(2,1)S(1)}) all-reduce(f32[512,512]{0,1:T(8,128)} %bitcast.69, f32[512,512]{0,1:T(8,128)} %bitcast.74), channel_id=1, replica_groups=mesh['seq'=64,'heads'=4] {'seq'}, use_global_device_ids=true, to_apply=%region_5.6 | all-reduce | flops 524288 | bytes 3145728 | tf_op jit(solution)/shard_map/psum | solution.py:75
  508.5 1.3 fusion.47
  509.8 0.3 copy-done.5
  510.0 2.6 add_convert_fusion
  512.7 0.0 all-reduce.5.cloned.1.call-start
  512.8 187.2 %all_gather.3 = bf16[512,512]{1,0:T(8,128)(2,1)S(1)} all-gather(bf16[8,512]{1,0:T(8,128)(2,1)S(1)} %copy-done.8), channel_id=1, replica_groups=mesh['seq'=64,'heads'=4] {'seq'}, dimensions={0}, use_global_device_ids=true | all-gather | bytes 532480 | tf_op jit(solution)/shard_map/all_gather | solution.py:34
  699.9 0.9 convolution_convert_fusion.1
  700.8 2.0 convolution_convert_fusion
  702.9 0.0 reduce-scatter.5.cloned.1.call-start
  702.9 38.1 %all-reduce.5.cloned.1.call-done = (bf16[512,128]{1,0:T(8,128)(2,1)}, bf16[512,128]{1,0:T(8,128)(2,1)}) async-done(((bf16[512,128]{1,0:T(8,128)(2,1)}, bf16[512,128]{1,0:T(8,128)(2,1)}), (bf16[512,128]{1,0:T(8,128)(2,1)}, bf16[512,128]{1,0:T(8,128)(2,1)})) %all-reduce.5.cloned.1.call-update) | async-done | bytes 262160 | tf_op jit(solution)/shard_map/psum | solution.py:90
  741.1 2.3 fusion.34
  743.3 3.3 copy.49
  746.6 384.8 %reduce-scatter.5.cloned.1.call-done = f32[8,512]{1,0:T(8,128)} async-done(((f32[512,512]{1,0:T(8,128)}), f32[8,512]{1,0:T(8,128)}) %reduce-scatter.5.cloned.1.call-update) | async-done | bytes 16400 | tf_op jit(solution)/shard_map/reduce_scatter | solution.py:94
  1131.4 1.3 convert_add_fusion
  (43 shorter events, 0.2 us)
Async XLA Ops:
  7.2 501.3 %copy-start = (bf16[2048,512]{1,0:T(8,128)(2,1)S(1)}, bf16[2048,512]{1,0:T(8,128)(2,1)}, u32[]{:S(2)}) copy-start(bf16[2048,512]{1,0:T(8,128)(2,1)} %param.15) | copy-start | bytes 6291460
  7.2 693.7 %reduce-scatter.3.cloned.1.call-start = ((), (), s32[]{:S(2)}) async-start(), calls=%async_computation.2 | async-start | bytes 2621440 | tf_op jit(solution)/shard_map/reduce_scatter | solution.py:76
  22.3 3.2 copy-start.2
  31.8 3.7 copy-start.1
  35.6 1.2 copy-start.3
  37.7 2.2 copy-start.4
  42.9 3.2 copy-start.2
  52.7 3.7 copy-start.1
  56.5 1.2 copy-start.3
  58.6 2.1 copy-start.4
  63.8 3.2 copy-start.2
  73.6 3.7 copy-start.1
  77.3 1.2 copy-start.3
  79.5 2.1 copy-start.4
  84.7 3.2 copy-start.2
  94.4 3.7 copy-start.1
  98.2 1.2 copy-start.3
  100.3 2.2 copy-start.4
  508.4 1.6 copy-start.5
  510.0 2.7 copy-start.8
  510.0 189.9 %copy-start.6 = (bf16[512,128]{1,0:T(8,128)(2,1)S(1)}, bf16[512,128]{1,0:T(8,128)(2,1)}, u32[]{:S(2)}) copy-start(bf16[512,128]{1,0:T(8,128)(2,1)} %param.18) | copy-start | bytes 393220
  510.0 190.8 %copy-start.7 = (bf16[128,512]{1,0:T(8,128)(2,1)S(1)}, bf16[128,512]{1,0:T(8,128)(2,1)}, u32[]{:S(2)}) copy-start(bf16[128,512]{1,0:T(8,128)(2,1)} %param.19) | copy-start | bytes 393220
  512.7 228.4 %all-reduce.5.cloned.1.call-start = ((), (), s32[]{:S(2)}) async-start(), calls=%async_computation.4 | async-start | bytes 524288 | tf_op jit(solution)/shard_map/psum | solution.py:90
  702.9 428.5 %reduce-scatter.5.cloned.1.call-start = ((), (), s32[]{:S(2)}) async-start(), calls=%async_computation.3 | async-start | bytes 1064960 | tf_op jit(solution)/shard_map/reduce_scatter | solution.py:94
Sparse Core Ops, SparseCore 0:
  512.8 27.8 reduce-scatter.2
  703.0 38.0 all-reduce.4
  743.6 387.8 reduce-scatter.4
where the time goes:
time: 1140 us
  blocking collectives  591 us (52%)
  waiting for transfers between devices  423 us (37%)
  matrix products  58.8 us (5%)
  local copies, waits for them, and re-layouts  31.5 us (3%)
  other arithmetic  21.1 us (2%)
  between operations  13.8 us (1%)
    psum x1, blocking collectives, local(): key_sum, value_sum = lax.psum((key_total, value_total), 'seq')  404 us
    reduce_scatter x1, waiting for transfers between devices, local(): lax.psum_scatter(input_part, 'seq', scatter_dimension=0, tiled=True)  385 us
    all_gather x1, blocking collectives, local(): lax.all_gather(global_in, 'seq', axis=0, tiled=True)  187 us
    psum x1, waiting for transfers between devices, local(): lax.psum(back_part.astype(jnp.bfloat16), 'heads').astype(jnp.float32)  38.1 us
    dot_general x4, matrix products, attend(): jnp.einsum('hrg,rhd->ghd', weights_low, grad_block, preferred_element_typ...  26.1 us
  transfers between devices with their start and end apart: 3, of which 2 were waited for; matrix products, arithmetic and copies ran while one was open for 0% of the time, Pallas kernels for 0%

commit v1 on v0

--- a/solution.py
+++ b/solution.py
@@ -31,7 +31,9 @@
     block = min(512, tok_rows)
     blocks = tok_rows // block
     pre_part = jnp.dot(
-        lax.all_gather(global_in, "seq", axis=0, tiled=True),
+        jnp.concatenate(
+            lax.all_to_all(jnp.stack([global_in] * lax.axis_size("seq")), "seq", 0, 0), axis=0
+        ),
         up_proj,
         preferred_element_type=jnp.float32,
     )

time: 1140 us -> 989 us (0.87)
  blocking collectives: 591 us -> 423 us
  waiting for transfers between devices: 423 us -> 440 us
    all_gather x1 -> x0, blocking collectives: 187 us -> none  [local(): lax.all_gather(global_in, 'seq', axis=0, tiled=True)]
    all_to_all x0 -> x1, blocking collectives: none -> 19.3 us  [local(): lax.all_to_all(jnp.stack([global_in] * lax.axis_size('seq')), 'seq', 0, 0)]
    reduce_scatter x1, waiting for transfers between devices: 0.01 us -> 11.9 us  [local(): lax.psum_scatter(project(key_sum, value_sum, key_proj, value_proj).astype...]
  transfers between devices with their start and end apart: 3 -> 3, of which waited for: 2 -> 3; matrix products, arithmetic and copies ran while one was open for 0% -> 0% of each run, Pallas kernels for 0% -> 0%
where the time goes in v1:
time: 989 us; the launch traced here: 988 us
  waiting for transfers between devices  440 us (44%)
  blocking collectives  423 us (43%)
  matrix products  58.8 us (6%)
  local copies, waits for them, and re-layouts  31.5 us (3%)
  other arithmetic  21.1 us (2%)
  between operations  13.8 us (1%)
    psum x1, blocking collectives, local(): key_sum, value_sum = lax.psum((key_total, value_total), 'seq')  404 us
    reduce_scatter x1, waiting for transfers between devices, local(): lax.psum_scatter(input_part, 'seq', scatter_dimension=0, tiled=True)  385 us
    psum x1, waiting for transfers between devices, local(): lax.psum(back_part.astype(jnp.bfloat16), 'heads').astype(jnp.float32)  42.7 us
    dot_general x4, matrix products, attend(): jnp.einsum('hrg,rhd->ghd', weights_low, grad_block, preferred_element_typ...  26.1 us
  transfers between devices with their start and end apart: 3, of which 3 were waited for; matrix products, arithmetic and copies ran while one was open for 0% of the time, Pallas kernels for 0%

profile of v1, /device:TPU:0, one launch (start us, length us, event | category | flops | bytes accessed | tf_op | source)
XLA Modules:
  0.0 988.0 jit_solution(10260480454568919851)
XLA Ops:
  7.2 0.0 reduce-scatter.3.cloned.1.call-start
  7.3 1.4 copy.22
  8.6 0.3 copy.25
  8.9 1.3 copy.23
  10.2 1.0 copy.27
  11.2 4.0 reshape.33
  15.2 4.0 reshape.35
  19.2 83.3 %while.15 = (s32[]{:T(128)}, f32[512,4,128]{0,2,1:T(8,128)}, f32[512,4,128]{0,2,1:T(8,128)}, bf16[4,512,4,128]{3,2,1,0:T(4,128)(2,1)}, bf16[4,512,4,128]{3,2,1,0...) while((s32[]{:T(128)}, f32[512,4,128]{0,2,1:T(8,128)}, ...), condition=%wide.region_4.5_spmd.clone, body=%wide.region_0.4_spmd.clone.sunk | while | flops 1360528384 | bytes 93372648 | solution.py:71
  19.2 2.4 constant_dynamic-slice_fusion.3
  21.5 0.7 fusion.81
  22.3 3.2 fusion.82
  25.5 6.4 fusion.84
  31.8 3.4 multiply_reduce_fusion.3
  35.2 0.4 copy-done.1
  35.6 1.2 multiply_convert_fusion.2
  36.8 0.9 fusion.83
  37.7 0.9 fusion.85
  38.6 1.2 copy_dynamic-update-slice_fusion.2
  39.9 2.4 constant_dynamic-slice_fusion.3
  42.2 0.7 fusion.81
  43.0 3.2 fusion.82
  46.1 6.6 fusion.84
  52.7 3.4 multiply_reduce_fusion.3
  56.1 0.4 copy-done.1
  56.5 1.2 multiply_convert_fusion.2
  57.7 0.9 fusion.83
  58.6 0.9 fusion.85
  59.5 1.2 copy_dynamic-update-slice_fusion.2
  60.7 2.4 constant_dynamic-slice_fusion.3
  63.1 0.7 fusion.81
  63.8 3.2 fusion.82
  67.0 6.6 fusion.84
  73.6 3.4 multiply_reduce_fusion.3
  77.0 0.4 copy-done.1
  77.3 1.2 multiply_convert_fusion.2
  78.6 0.9 fusion.83
  79.5 0.9 fusion.85
  80.4 1.2 copy_dynamic-update-slice_fusion.2
  81.6 2.4 constant_dynamic-slice_fusion.3
  84.0 0.7 fusion.81
  84.7 3.2 fusion.82
  87.9 6.6 fusion.84
  94.4 3.4 multiply_reduce_fusion.3
  97.8 0.4 copy-done.1
  98.2 1.2 multiply_convert_fusion.2
  99.4 0.9 fusion.83
  100.3 0.9 fusion.85
  101.3 1.2 copy_dynamic-update-slice_fusion.2
  102.5 2.3 broadcast_multiply_fusion
  104.8 403.7 %all-reduce.6 = (bf16[512,512]{0,1:T(8,128)(2,1)S(1)}, bf16[512,512]{0,1:T(8,128)(2,1)S(1)}) all-reduce(f32[512,512]{0,1:T(8,128)} %bitcast.71, f32[512,512]{0,1:T(8,128)} %bitcast.76), channel_id=1, replica_groups=mesh['seq'=64,'heads'=4] {'seq'}, use_global_device_ids=true, to_apply=%region_5.6 | all-reduce | flops 524288 | bytes 3145728 | tf_op jit(solution)/shard_map/psum | solution.py:77
  508.5 1.3 fusion.48
  509.8 0.3 copy-done.5
  510.1 2.6 add_convert_fusion
  512.7 0.0 all-reduce.5.cloned.1.call-start
  512.8 19.3 %all_to_all.5 = bf16[64,8,512]{2,1,0:T(8,128)(2,1)S(1)} all-to-all(bf16[64,8,512]{2,1,0:T(8,128)(2,1)S(1)} %stack.2), channel_id=1, replica_groups=mesh['seq'=64,'heads'=4] {'seq'}, dimensions={0} | all-to-all | bytes 1048576 | tf_op jit(solution)/shard_map/all_to_all | solution.py:35
  532.1 0.9 convolution_convert_fusion.1
  533.1 11.9 %reduce-scatter.3.cloned.1.call-done = bf16[512,512]{1,0:T(8,128)(2,1)} async-done(((bf16[512,2048]{1,0:T(8,128)(2,1)}), bf16[512,512]{1,0:T(8,128)(2,1)}) %reduce-scatter.3.cloned.1.call-update) | async-done | bytes 524304 | tf_op jit(solution)/shard_map/reduce_scatter | solution.py:78
  545.0 2.0 convolution_convert_fusion
  547.0 0.0 reduce-scatter.5.cloned.1.call-start
  547.0 42.7 %all-reduce.5.cloned.1.call-done = (bf16[512,128]{1,0:T(8,128)(2,1)}, bf16[512,128]{1,0:T(8,128)(2,1)}) async-done(((bf16[512,128]{1,0:T(8,128)(2,1)}, bf16[512,128]{1,0:T(8,128)(2,1)}), (bf16[512,128]{1,0:T(8,128)(2,1)}, bf16[512,128]{1,0:T(8,128)(2,1)})) %all-reduce.5.cloned.1.call-update) | async-done | bytes 262160 | tf_op jit(solution)/shard_map/psum | solution.py:92
  589.7 2.3 fusion.35
  592.0 3.3 copy.49
  595.3 384.9 %reduce-scatter.5.cloned.1.call-done = f32[8,512]{1,0:T(8,128)} async-done(((f32[512,512]{1,0:T(8,128)}), f32[8,512]{1,0:T(8,128)}) %reduce-scatter.5.cloned.1.call-update) | async-done | bytes 16400 | tf_op jit(solution)/shard_map/reduce_scatter | solution.py:96
  980.2 1.3 convert_add_fusion
  (44 shorter events, 0.3 us)
Async XLA Ops:
  7.2 501.3 %copy-start = (bf16[2048,512]{1,0:T(8,128)(2,1)S(1)}, bf16[2048,512]{1,0:T(8,128)(2,1)}, u32[]{:S(2)}) copy-start(bf16[2048,512]{1,0:T(8,128)(2,1)} %param.15) | copy-start | bytes 6291460
  7.2 537.8 %reduce-scatter.3.cloned.1.call-start = ((), (), s32[]{:S(2)}) async-start(), calls=%async_computation.3 | async-start | bytes 2621440 | tf_op jit(solution)/shard_map/reduce_scatter | solution.py:78
  22.3 3.2 copy-start.2
  31.8 3.7 copy-start.1
  35.6 1.2 copy-start.3
  37.7 2.2 copy-start.4
  42.9 3.2 copy-start.2
  52.7 3.7 copy-start.1
  56.5 1.2 copy-start.3
  58.6 2.1 copy-start.4
  63.8 3.2 copy-start.2
  73.6 3.7 copy-start.1
  77.3 1.2 copy-start.3
  79.5 2.1 copy-start.4
  84.7 3.2 copy-start.2
  94.4 3.7 copy-start.1
  98.2 1.2 copy-start.3
  100.3 2.2 copy-start.4
  508.5 1.6 copy-start.5
  510.1 2.7 copy-start.8
  510.1 22.1 %copy-start.6 = (bf16[512,128]{1,0:T(8,128)(2,1)S(1)}, bf16[512,128]{1,0:T(8,128)(2,1)}, u32[]{:S(2)}) copy-start(bf16[512,128]{1,0:T(8,128)(2,1)} %param.18) | copy-start | bytes 393220
  512.7 32.3 %copy-start.7 = (bf16[128,512]{1,0:T(8,128)(2,1)S(1)}, bf16[128,512]{1,0:T(8,128)(2,1)}, u32[]{:S(2)}) copy-start(bf16[128,512]{1,0:T(8,128)(2,1)} %param.19) | copy-start | bytes 393220
  512.7 77.0 %all-reduce.5.cloned.1.call-start = ((), (), s32[]{:S(2)}) async-start(), calls=%async_computation.5 | async-start | bytes 524288 | tf_op jit(solution)/shard_map/psum | solution.py:92
  547.0 433.2 %reduce-scatter.5.cloned.1.call-start = ((), (), s32[]{:S(2)}) async-start(), calls=%async_computation.4 | async-start | bytes 1064960 | tf_op jit(solution)/shard_map/reduce_scatter | solution.py:96
Sparse Core Ops, SparseCore 0:
  512.9 32.0 reduce-scatter.2
  548.2 41.4 all-reduce.4
  592.2 387.9 reduce-scatter.4
